TPU v7x, 512 devices: a whole 4x8x8 slice. The times are simulated.
512 devices in a mesh: tok: 64 (over y, z_lo, x), feat: 8 (over z_hi, core).
Axes of the slice: x: 4, y: 8, z: 8 (z_hi: 4, z_lo: 2; z = z_hi * 2 + z_lo), core: 2. Of those that a mesh axis runs over, the one named last changes fastest.
Arguments:
- hidden_states: bfloat16 [110592, 8192], P('tok', 'feat'), may hold values from -60 to 60
- current_block: float32 [8192, 64], P('feat'), may hold values from -0.0625 to 0.0625
- directions: float32 [8192, 64], P('feat'), may hold values from -0.0625 to 0.0625
Outputs:
- block_image: float32 [8192, 192], P('feat')
- gram_image: float32 [192, 192], replicated
- gram_search: float32 [192, 192], replicated
All inputs are finite; a program needn't handle non-finite values.
Results may differ from a plain program's by a relative error of at most 0.005.
Values may be sent and summed in bfloat16 or wider, within the bound.
No kernel may reach another device: no remote copies, remote signals or barrier semaphores. Data moves between devices by JAX's collectives and lax.ppermute only.
A program may use at most 64 MiB of HBM per device.

v0:
```python
import math
import jax
import jax.numpy as jnp
from jax import lax
from jax.sharding import PartitionSpec as P

LAG = 256
SMALL = 2.0 ** (-20)
HIGHEST = lax.Precision.HIGHEST


def exchange(value, axis):
    return lax.all_to_all(value, axis, 0, 0, tiled=True)


def scattered_sum(value, axis):
    return jnp.sum(exchange(value, axis).astype(jnp.float32), axis=0)


def gathered(value, axis):
    return exchange(jnp.broadcast_to(value, (lax.axis_size(axis),) + value.shape), axis)


def rows_dot(a, b, **kwargs):
    return lax.dot_general(
        a, b, (((1,), (1,)), ((), ())), preferred_element_type=jnp.float32, **kwargs
    )


def local(hidden_states, current_block, directions):
    tokens, features = hidden_states.shape
    cols = current_block.shape[1]
    feat, tok = (lax.axis_size("feat"), lax.axis_size("tok"))
    factor = 0.5 / math.sqrt(tokens * tok - LAG)
    half = jnp.bfloat16
    up = [(i, i + 1) for i in range(tok - 1)]
    down = [(i + 1, i) for i in range(tok - 1)]
    behind = lax.ppermute(hidden_states[tokens - LAG :], "tok", up)
    ahead = lax.ppermute(hidden_states[:LAG], "tok", down)
    x, p = (current_block.T, directions.T)

    def project(vectors):
        pieces = [rows_dot(vectors, part) for part in (behind, hidden_states, ahead)]
        return jnp.concatenate(pieces, axis=1)

    def lagged(projected):
        return projected[:, 2 * LAG :] + projected[:, :tokens]

    def backward(lagged_rows):
        return lax.dot_general(
            lagged_rows, hidden_states, (((1,), (0,)), ((), ())), preferred_element_type=jnp.float32
        )

    side = lax.psum(
        jnp.concatenate(
            [
                project(p.astype(half)),
                rows_dot(p, jnp.concatenate([x, p]), precision=HIGHEST),
                rows_dot(x, x, precision=HIGHEST),
            ],
            axis=1,
        ),
        "feat",
    )
    part = lagged(project(x.astype(half)))
    own = scattered_sum(part.reshape(feat, cols // feat, tokens), "feat").astype(half)
    lag_x = gathered(own, "feat").reshape(cols, tokens)
    own = scattered_sum(backward(lag_x).reshape(tok, cols // tok, features), "tok") * factor
    image_x = gathered(own, "tok").reshape(cols, features)
    both = rows_dot(image_x, jnp.concatenate([x, p]), precision=HIGHEST)
    both = jnp.sum(gathered(both, "feat"), axis=0)
    rayleigh_t, image_x_p = (both[:, :cols], both[:, cols:])
    residual = (image_x - jnp.dot(rayleigh_t, x, precision=HIGHEST)) * SMALL
    width = tokens + 2 * LAG
    part = jnp.concatenate(
        [
            project(residual.astype(half)),
            rows_dot(residual, jnp.concatenate([x, residual, p]), precision=HIGHEST),
        ],
        axis=1,
    )
    own = scattered_sum(part.reshape(feat, cols // feat, part.shape[1]), "feat")
    high = own.astype(half)
    low = (own[:, width:] - high[:, width:].astype(jnp.float32)).astype(half)
    everything = gathered(jnp.concatenate([high, low], axis=1), "feat").reshape(cols, -1)
    proj_r = everything[:, :width]
    inner = everything[:, width:].astype(jnp.float32)
    inner = inner[:, : 3 * cols] + inner[:, 3 * cols :]
    r_x, r_r, r_p = (inner[:, i * cols : (i + 1) * cols] for i in range(3))
    proj_p = side[:, :width]
    lag_r = lagged(proj_r.astype(jnp.float32)).astype(half)
    lag_p = lagged(proj_p).astype(half)
    mid_r = proj_r[:, LAG : LAG + tokens]
    mid_p = proj_p[:, LAG : LAG + tokens].astype(half)
    image = backward(jnp.concatenate([lag_r, lag_p]))
    cross = rows_dot(jnp.concatenate([mid_r, mid_p]), jnp.concatenate([lag_r, lag_p]))
    part = jnp.concatenate(
        [
            image[:cols].reshape(tok, -1),
            image[cols:].reshape(tok, -1),
            cross[:cols, :cols].reshape(tok, -1),
            cross[cols:, :cols].reshape(tok, -1),
            cross[cols:, cols:].reshape(tok, -1),
        ],
        axis=1,
    )
    own = scattered_sum(part[:, None, :], "tok") * factor
    total = gathered(own, "tok")[:, 0, :]
    sizes = [cols * features // tok] * 2 + [cols * cols // tok] * 3
    ends = [sum(sizes[: i + 1]) for i in range(5)]
    image_r, image_p = (
        total[:, e - s : e].reshape(cols, features) for e, s in zip(ends[:2], sizes[:2])
    )
    c_rr, c_pr, c_pp = (
        total[:, e - s : e].reshape(cols, cols) for e, s in zip(ends[2:], sizes[2:])
    )
    lengths = jnp.sum(r_r * jnp.eye(cols, dtype=jnp.float32), axis=1, keepdims=True)
    scale = lax.rsqrt(lengths * (1.0 / SMALL**2) + 1e-06) * (1.0 / SMALL)
    across = scale.T
    block_image = jnp.concatenate([image_x, image_r * scale, image_p])
    u_x, u_p = (r_x * scale, r_p * scale)
    u_u = r_r * scale * across
    u_image_x = (r_r * (1.0 / SMALL) + jnp.dot(r_x, rayleigh_t.T, precision=HIGHEST)) * scale
    p_image_u = c_pr * across
    gram_image = jnp.concatenate(
        [
            jnp.concatenate([rayleigh_t.T, u_image_x.T, image_x_p], axis=1),
            jnp.concatenate([u_image_x, c_rr * scale * across, p_image_u.T], axis=1),
            jnp.concatenate([image_x_p.T, p_image_u, c_pp], axis=1),
        ]
    )
    p_x, p_p, x_x = (side[:, width + i * cols : width + (i + 1) * cols] for i in range(3))
    gram_search = jnp.concatenate(
        [
            jnp.concatenate([x_x, u_x.T, p_x.T], axis=1),
            jnp.concatenate([u_x, u_u, u_p], axis=1),
            jnp.concatenate([p_x, u_p.T, p_p], axis=1),
        ]
    )
    return (block_image.T, gram_image, gram_search)


def solution(mesh):
    return jax.shard_map(
        local,
        mesh=mesh,
        in_specs=(P("tok", "feat"), P("feat", None), P("feat", None)),
        out_specs=(P("feat", None), P(), P()),
        check_vma=False,
    )
```

profile of v0, /device:TPU:8, one launch (start us, length us, event | category | flops | bytes accessed | tf_op | source)
XLA Modules:
  0.0 323.3 jit_solution(342067930068575905)
XLA Ops:
  7.2 1.3 fusion.44
  8.5 3.4 %collective-permute-start.1 = (bf16[256,1024]{1,0:T(8,128)(2,1)S(1)}, bf16[256,1024]{1,0:T(8,128)(2,1)S(1)}, u32[]{:S(2)}, u32[]{:S(2)}) collective-permute-start(bf16[256,1024]{1,0:T(8,128)(2,1)S(1)} %get-tuple-element.16), channel_id=1, source_target_pairs={{0,8},{8,16},{16,24},{24,32},{32,40},{40,48},{48,56},{56,64},{64,7... | collective-permute-start | bytes 1572872 | tf_op jit(solution)/shard_map/ppermute | solution.py:38
  11.9 5.5 %collective-permute-start = (bf16[256,1024]{1,0:T(8,128)(2,1)S(1)}, bf16[256,1024]{1,0:T(8,128)(2,1)S(1)}, u32[]{:S(2)}, u32[]{:S(2)}) collective-permute-start(bf16[256,1024]{1,0:T(8,128)(2,1)S(1)} %get-tuple-element.15), channel_id=1, source_target_pairs={{8,0},{16,8},{24,16},{32,24},{40,32},{48,40},{56,48},{64,56},{72,6... | collective-permute-start | bytes 1572872 | tf_op jit(solution)/shard_map/ppermute | solution.py:39
  17.4 3.2 fusion.49
  20.6 6.5 %collective-permute-done.1 = bf16[256,1024]{1,0:T(8,128)(2,1)S(1)} collective-permute-done((bf16[256,1024]{1,0:T(8,128)(2,1)S(1)}, bf16[256,1024]{1,0:T(8,128)(2,1)S(1)}, u32[]{:S(2)}, u32[]{:S(2)}) %collective-permute-start.1) | collective-permute-done | bytes 524320 | tf_op jit(solution)/shard_map/ppermute | solution.py:38
  27.3 0.9 collective-permute-done
  29.2 26.6 %all_to_all.45 = f32[8,8,1728]{2,1,0:T(8,128)} all-to-all(f32[8,8,1728]{2,1,0:T(8,128)S(1)} %fusion.12), channel_id=1, replica_groups=mesh['tok'=64,'feat'=8] {'feat'}, dimensions={0} | all-to-all | bytes 884736 | tf_op jit(solution)/shard_map/all_to_all | solution.py:13
  55.8 1.7 reduce_sum.54
  58.2 14.3 %all_to_all.46 = bf16[8,8,1728]{2,1,0:T(8,128)(2,1)S(1)} all-to-all(bf16[8,8,1728]{2,1,0:T(8,128)(2,1)S(1)} %broadcast_in_dim.19), channel_id=1, replica_groups=mesh['tok'=64,'feat'=8] {'feat'}, dimensions={0} | all-to-all | bytes 442368 | tf_op jit(solution)/shard_map/all_to_all | solution.py:13
  73.5 22.8 %all_to_all.47 = f32[64,1,1024]{2,1,0:T(1,128)} all-to-all(f32[64,1,1024]{2,1,0:T(1,128)S(1)} %copy.65), channel_id=1, replica_groups=mesh['tok'=64,'feat'=8] {'tok'}, dimensions={0} | all-to-all | bytes 524288 | tf_op jit(solution)/shard_map/all_to_all | solution.py:13
  96.4 1.1 reduce_sum.55
  97.7 16.2 %all_to_all.48 = f32[64,1,1024]{2,1,0:T(1,128)S(1)} all-to-all(f32[64,1,1024]{2,1,0:T(1,128)S(1)} %broadcast_in_dim.20), channel_id=1, replica_groups=mesh['tok'=64,'feat'=8] {'tok'}, dimensions={0} | all-to-all | bytes 524288 | tf_op jit(solution)/shard_map/all_to_all | solution.py:13
  114.5 1.7 fusion.17
  116.3 16.4 %all_to_all.49 = f32[8,64,128]{2,1,0:T(8,128)} all-to-all(f32[8,64,128]{2,1,0:T(8,128)S(1)} %broadcast_in_dim.21), channel_id=1, replica_groups=mesh['tok'=64,'feat'=8] {'feat'}, dimensions={0} | all-to-all | bytes 524288 | tf_op jit(solution)/shard_map/all_to_all | solution.py:13
  132.6 1.6 reduce_sum.56
  134.2 1.4 fusion
  135.7 2.0 fusion.32
  137.6 1.5 fusion.5
  139.2 0.9 fusion.34
  140.1 0.9 fusion.30
  141.0 2.0 concatenate.65
  143.0 4.2 %all-to-all-start.5 = ((f32[8,8,2432]{2,1,0:T(8,128)}), f32[8,8,2432]{2,1,0:T(8,128)}, u32[]{:S(2)}, u32[]{:S(2)}) async-start(f32[8,8,2432]{2,1,0:T(8,128)} %bitcast.123), calls=%async_computation.5 | async-start | bytes 1245184 | tf_op jit(solution)/shard_map/all_to_all | solution.py:13
  147.2 2.1 convolution_dynamic-update-slice_fusion.2
  149.3 3.0 convolution_dynamic-update-slice_fusion
  152.3 0.9 convolution_dynamic-update-slice_fusion.1
  153.2 1.2 fusion.1
  154.4 1.0 convolution_dynamic-update-slice_fusion.3
  155.4 11.6 %all-to-all-done.5 = f32[8,8,2432]{2,1,0:T(8,128)} async-done(((f32[8,8,2432]{2,1,0:T(8,128)}), f32[8,8,2432]{2,1,0:T(8,128)}, u32[]{:S(2)}, u32[]{:S(2)}) %all-to-all-start.5) | async-done | bytes 622624 | tf_op jit(solution)/shard_map/all_to_all | solution.py:13
  167.0 1.7 reduce_sum.57
  168.7 0.9 convert_element_type.38
  171.2 4.3 %all-to-all-start.6 = ((bf16[8,8,2624]{2,1,0:T(8,128)(2,1)}), bf16[8,8,2624]{2,1,0:T(8,128)(2,1)}, u32[]{:S(2)}, u32[]{:S(2)}) async-start(bf16[8,8,2624]{2,1,0:T(8,128)(2,1)} %broadcast_in_dim.22), calls=%async_computation.6 | async-start | bytes 688128 | tf_op jit(solution)/shard_map/all_to_all | solution.py:13
  175.4 65.7 %all-reduce.2.cloned.1.call-done = f32[64,2432]{0,1:T(8,128)} async-done(((f32[64,2432]{0,1:T(8,128)}), f32[64,2432]{0,1:T(8,128)}) %all-reduce.2.cloned.1.call-update) | async-done | bytes 622608 | tf_op jit(solution)/shard_map/psum | solution.py:54
  241.1 2.0 slice.200
  243.1 2.3 fusion.3
  245.4 1.7 slice.145
  247.1 1.7 slice.152
  248.7 2.0 copy.96
  250.7 1.1 convert_element_type.41
  251.9 0.8 fusion.4
  252.7 1.9 copy.97
  254.6 2.2 fusion.19
  258.4 28.5 %all_to_all.50 = f32[64,1,2240]{2,1,0:T(1,128)S(1)} all-to-all(f32[64,1,2240]{2,1,0:T(1,128)S(1)} %copy.74), channel_id=1, replica_groups=mesh['tok'=64,'feat'=8] {'tok'}, dimensions={0} | all-to-all | bytes 1146880 | tf_op jit(solution)/shard_map/all_to_all | solution.py:13
  287.3 1.1 broadcast_in_dim.24
  288.4 6.2 %all-to-all-start.8 = ((f32[64,1,2240]{2,1,0:T(1,128)}), f32[64,1,2240]{2,1,0:T(1,128)S(1)}, u32[]{:S(2)}, u32[]{:S(2)}) async-start(f32[64,1,2240]{2,1,0:T(1,128)} %broadcast_in_dim.24), calls=%async_computation.8 | async-start | bytes 1179648 | tf_op jit(solution)/shard_map/all_to_all | solution.py:13
  294.9 0.9 slice.157
  296.3 15.7 %all-to-all-done.8 = f32[64,1,2240]{2,1,0:T(1,128)S(1)} async-done(((f32[64,1,2240]{2,1,0:T(1,128)}), f32[64,1,2240]{2,1,0:T(1,128)S(1)}, u32[]{:S(2)}, u32[]{:S(2)}) %all-to-all-start.8) | async-done | bytes 573472 | tf_op jit(solution)/shard_map/all_to_all | solution.py:13
  312.4 0.9 slice_multiply_fusion.2
  314.8 0.9 maximum_bitcast_fusion
  (84 shorter events, 10.6 us)
Async XLA Ops:
  7.2 10.2 %copy-start.1 = (f32[1024,64]{0,1:T(8,128)S(1)}, f32[1024,64]{0,1:T(8,128)}, u32[]{:S(2)}) copy-start(f32[1024,64]{0,1:T(8,128)} %param.4) | copy-start | bytes 786436
  8.5 18.6 %collective-permute-start.1 = (bf16[256,1024]{1,0:T(8,128)(2,1)S(1)}, bf16[256,1024]{1,0:T(8,128)(2,1)S(1)}, u32[]{:S(2)}, u32[]{:S(2)}) collective-permute-start(bf16[256,1024]{1,0:T(8,128)(2,1)S(1)} %get-tuple-element.16), channel_id=1, source_target_pairs={{0,8},{8,16},{16,24},{24,32},{32,40},{40,48},{48,56},{56,64},{64,7... | collective-permute-start | bytes 1572872 | tf_op jit(solution)/shard_map/ppermute | solution.py:38
  11.9 16.3 %collective-permute-start = (bf16[256,1024]{1,0:T(8,128)(2,1)S(1)}, bf16[256,1024]{1,0:T(8,128)(2,1)S(1)}, u32[]{:S(2)}, u32[]{:S(2)}) collective-permute-start(bf16[256,1024]{1,0:T(8,128)(2,1)S(1)} %get-tuple-element.15), channel_id=1, source_target_pairs={{8,0},{16,8},{24,16},{32,24},{40,32},{48,40},{56,48},{64,56},{72,6... | collective-permute-start | bytes 1572872 | tf_op jit(solution)/shard_map/ppermute | solution.py:39
  27.1 2.1 copy-start.6
  28.2 0.8 copy-start.8
  28.2 44.3 %copy-start = (bf16[1728,1024]{1,0:T(8,128)(2,1)S(1)}, bf16[1728,1024]{1,0:T(8,128)(2,1)}, u32[]{:S(2)}) copy-start(bf16[1728,1024]{1,0:T(8,128)(2,1)} %param.3) | copy-start | bytes 10616836
  113.8 0.7 copy-start.11
  135.6 2.0 copy-start.2
  135.7 2.0 copy-start.4
  137.6 1.5 copy-start.7
  137.6 2.4 copy-start.9
  143.0 24.0 %all-to-all-start.5 = ((f32[8,8,2432]{2,1,0:T(8,128)}), f32[8,8,2432]{2,1,0:T(8,128)}, u32[]{:S(2)}, u32[]{:S(2)}) async-start(f32[8,8,2432]{2,1,0:T(8,128)} %bitcast.123), calls=%async_computation.5 | async-start | bytes 1245184 | tf_op jit(solution)/shard_map/all_to_all | solution.py:13
  147.2 93.9 %all-reduce.2.cloned.1.call-start = ((), (), s32[]{:S(2)}) async-start(), calls=%async_computation.9 | async-start | bytes 2490368 | tf_op jit(solution)/shard_map/psum | solution.py:54
  149.3 3.0 copy-start.5
  149.3 3.0 copy-start.10
  149.3 4.0 %copy-start.3 = (f32[1024,64]{0,1:T(8,128)S(1)}, f32[1024,64]{0,1:T(8,128)}, u32[]{:S(2)}) copy-start(f32[1024,64]{0,1:T(8,128)} %param.4) | copy-start | bytes 786436
  171.2 74.2 %all-to-all-start.6 = ((bf16[8,8,2624]{2,1,0:T(8,128)(2,1)}), bf16[8,8,2624]{2,1,0:T(8,128)(2,1)}, u32[]{:S(2)}, u32[]{:S(2)}) async-start(bf16[8,8,2624]{2,1,0:T(8,128)(2,1)} %broadcast_in_dim.22), calls=%async_computation.6 | async-start | bytes 688128 | tf_op jit(solution)/shard_map/all_to_all | solution.py:13
  254.6 2.3 copy-start.13
  254.6 2.3 copy-start.14
  254.6 2.3 copy-start.15
  254.6 2.3 copy-start.16
  286.9 7.7 %copy-start.12 = (f32[64,1,1024]{2,1,0:T(1,128)S(1)}, f32[64,1,1024]{2,1,0:T(1,128)}, u32[]{:S(2)}) copy-start(f32[64,1,1024]{2,1,0:T(1,128)} %copy-done.11) | copy-start | bytes 786436
  287.3 7.4 %copy-start.17 = (f32[64,128]{1,0:T(8,128)S(1)}, f32[64,128]{1,0:T(8,128)}, u32[]{:S(2)}) copy-start(f32[64,128]{1,0:T(8,128)} %reduce_sum.56) | copy-start | bytes 98308
  288.4 23.7 %all-to-all-start.8 = ((f32[64,1,2240]{2,1,0:T(1,128)}), f32[64,1,2240]{2,1,0:T(1,128)S(1)}, u32[]{:S(2)}, u32[]{:S(2)}) async-start(f32[64,1,2240]{2,1,0:T(1,128)} %broadcast_in_dim.24), calls=%async_computation.8 | async-start | bytes 1179648 | tf_op jit(solution)/shard_map/all_to_all | solution.py:13
Sparse Core Ops, SparseCore 0:
  155.5 85.4 all-reduce.1
where the time goes:
time: 325 us; the launch traced here: 323 us
  blocking collectives  125 us (38%)
  waiting for transfers between devices  100 us (31%)
  matrix products  24.1 us (7%)
  starting transfers between devices  23.6 us (7%)
  local copies, waits for them, and re-layouts  20.5 us (6%)
  other arithmetic  15.5 us (5%)
  between operations  14.4 us (4%)
    all_to_all x6, blocking collectives, exchange(): return lax.all_to_all(value, axis, 0, 0, tiled=True)  125 us
    psum x1, waiting for transfers between devices, local(): lax.psum(jnp.concatenate([project(p.astype(half)), rows_dot(p, jnp.concat...  65.7 us
    all_to_all x3, waiting for transfers between devices, exchange(): return lax.all_to_all(value, axis, 0, 0, tiled=True)  27.3 us
    dot_general x14, matrix products, rows_dot(): lax.dot_general(a, b, (((1,), (1,)), ((), ())), preferred_element_type=jn...  19.6 us
    all_to_all x3, starting transfers between devices, exchange(): return lax.all_to_all(value, axis, 0, 0, tiled=True)  14.7 us
    unnamed x47, local copies, waits for them, and re-layouts  6.63 us
  transfers between devices with their start and end apart: 6, of which 5 were waited for; matrix products, arithmetic and copies ran while one was open for 7% of the time, Pallas kernels for 0%

commit v1 on v0

--- a/solution.py
+++ b/solution.py
@@ -51,17 +51,15 @@
             lagged_rows, hidden_states, (((1,), (0,)), ((), ())), preferred_element_type=jnp.float32
         )
 
-    side = lax.psum(
-        jnp.concatenate(
-            [
-                project(p.astype(half)),
-                rows_dot(p, jnp.concatenate([x, p]), precision=HIGHEST),
-                rows_dot(x, x, precision=HIGHEST),
-            ],
-            axis=1,
-        ),
-        "feat",
+    frame_in = jnp.concatenate(
+        [
+            project(p.astype(half)),
+            rows_dot(p, jnp.concatenate([x, p]), precision=HIGHEST),
+            rows_dot(x, x, precision=HIGHEST),
+        ],
+        axis=1,
     )
+    side = jnp.sum(jax.lax.all_gather(frame_in, axis_name="feat"), axis=0)
     part = lagged(project(x.astype(half)))
     own = scattered_sum(part.reshape(feat, cols // feat, tokens), "feat").astype(half)
     lag_x = gathered(own, "feat").reshape(cols, tokens)

time: 325 us -> 289 us (0.89)
  waiting for transfers between devices: 100 us -> 34.9 us
  blocking collectives: 125 us -> 156 us
  local copies, waits for them, and re-layouts: 20.5 us -> 16.1 us
    psum x1 -> x0, waiting for transfers between devices: 65.7 us -> none  [local(): lax.psum(jnp.concatenate([project(p.astype(half)), rows_dot(p, jnp.concat...]
    all_to_all x6 -> x7, blocking collectives: 125 us -> 156 us  [exchange(): return lax.all_to_all(value, axis, 0, 0, tiled=True)]
    all_to_all x3 -> x2, waiting for transfers between devices: 27.3 us -> 33.7 us  [exchange(): return lax.all_to_all(value, axis, 0, 0, tiled=True)]
    ppermute x1, waiting for transfers between devices: 6.49 us -> 1.24 us  [local(): behind = lax.ppermute(hidden_states[tokens - LAG:], 'tok', up)]
    dot_general x14, matrix products: 19.6 us -> 23.4 us  [rows_dot(): lax.dot_general(a, b, (((1,), (1,)), ((), ())), preferred_element_type=jn...]
    reduce_sum x0 -> x1, other arithmetic: none -> 3.54 us  [local(): side = jnp.sum(jax.lax.all_gather(frame_in, axis_name='feat'), axis=0)]
    unnamed x47 -> x29, local copies, waits for them, and re-layouts: 6.63 us -> 3.56 us
    all_to_all x3 -> x2, starting transfers between devices: 14.7 us -> 12 us  [exchange(): return lax.all_to_all(value, axis, 0, 0, tiled=True)]
  transfers between devices with their start and end apart: 6 -> 5, of which waited for: 5 -> 3; matrix products, arithmetic and copies ran while one was open for 7% -> 14% of each run, Pallas kernels for 0% -> 0%
where the time goes in v1:
time: 289 us; the launch traced here: 288 us
  blocking collectives  156 us (54%)
  waiting for transfers between devices  34.9 us (12%)
  matrix products  27.3 us (9%)
  starting transfers between devices  21 us (7%)
  other arithmetic  18.3 us (6%)
  local copies, waits for them, and re-layouts  16.1 us (6%)
  between operations  14.4 us (5%)
    all_to_all x7, blocking collectives, exchange(): return lax.all_to_all(value, axis, 0, 0, tiled=True)  156 us
    all_to_all x2, waiting for transfers between devices, exchange(): return lax.all_to_all(value, axis, 0, 0, tiled=True)  33.7 us
    dot_general x14, matrix products, rows_dot(): lax.dot_general(a, b, (((1,), (1,)), ((), ())), preferred_element_type=jn...  23.4 us
    all_to_all x2, starting transfers between devices, exchange(): return lax.all_to_all(value, axis, 0, 0, tiled=True)  12 us
  transfers between devices with their start and end apart: 5, of which 3 were waited for; matrix products, arithmetic and copies ran while one was open for 14% of the time, Pallas kernels for 0%

profile of v1, /device:TPU:8, one launch (start us, length us, event | category | flops | bytes accessed | tf_op | source)
XLA Modules:
  0.0 288.1 jit_solution(17448575841425468818)
XLA Ops:
  7.2 1.4 fusion.47
  8.7 3.4 %collective-permute-start.1 = (bf16[256,1024]{1,0:T(8,128)(2,1)S(1)}, bf16[256,1024]{1,0:T(8,128)(2,1)S(1)}, u32[]{:S(2)}, u32[]{:S(2)}) collective-permute-start(bf16[256,1024]{1,0:T(8,128)(2,1)S(1)} %get-tuple-element.16), channel_id=1, source_target_pairs={{0,8},{8,16},{16,24},{24,32},{32,40},{40,48},{48,56},{56,64},{64,7... | collective-permute-start | bytes 1572872 | tf_op jit(solution)/shard_map/ppermute | solution.py:38
  12.1 5.6 %collective-permute-start = (bf16[256,1024]{1,0:T(8,128)(2,1)S(1)}, bf16[256,1024]{1,0:T(8,128)(2,1)S(1)}, u32[]{:S(2)}, u32[]{:S(2)}) collective-permute-start(bf16[256,1024]{1,0:T(8,128)(2,1)S(1)} %get-tuple-element.15), channel_id=1, source_target_pairs={{8,0},{16,8},{24,16},{32,24},{40,32},{48,40},{56,48},{64,56},{72,6... | collective-permute-start | bytes 1572872 | tf_op jit(solution)/shard_map/ppermute | solution.py:39
  17.7 4.1 %fusion.58 = f32[64,1728]{1,0:T(8,128)} fusion(bf16[1728,1024]{1,0:T(8,128)(2,1)} %param.3, f32[1024,64]{0,1:T(8,128)} %param.5), kind=kOutput, calls=%fused_computation.90 | convolution fusion | flops 226492416 | bytes 4243456 | tf_op jit(solution)/shard_map/dot_general | solution.py:25
  21.7 2.0 fusion.50
  23.7 1.3 convolution_bitcast_fusion.1
  25.0 1.0 fusion.68
  26.0 1.2 collective-permute-done.1
  28.0 0.9 fusion.56
  28.9 0.8 copy-done.4
  29.7 0.9 fusion.60
  30.7 2.0 concatenate.67
  32.6 1.4 fusion.54
  34.0 1.4 fusion.52
  35.5 1.2 fusion.11
  36.7 28.0 %all_to_all.45 = f32[8,8,1728]{2,1,0:T(8,128)} all-to-all(f32[8,8,1728]{2,1,0:T(8,128)S(1)} %fusion.11), channel_id=1, replica_groups=mesh['tok'=64,'feat'=8] {'feat'}, dimensions={0} | all-to-all | bytes 884736 | tf_op jit(solution)/shard_map/all_to_all | solution.py:13
  64.7 1.7 reduce_sum.63
  67.2 32.5 %all_to_all.46 = bf16[8,8,1728]{2,1,0:T(8,128)(2,1)S(1)} all-to-all(bf16[8,8,1728]{2,1,0:T(8,128)(2,1)S(1)} %broadcast_in_dim.19), channel_id=1, replica_groups=mesh['tok'=64,'feat'=8] {'feat'}, dimensions={0} | all-to-all | bytes 442368 | tf_op jit(solution)/shard_map/all_to_all | solution.py:13
  100.7 20.0 %all_to_all.47 = f32[64,1,1024]{2,1,0:T(1,128)} all-to-all(f32[64,1,1024]{2,1,0:T(1,128)S(1)} %copy.47), channel_id=1, replica_groups=mesh['tok'=64,'feat'=8] {'tok'}, dimensions={0} | all-to-all | bytes 524288 | tf_op jit(solution)/shard_map/all_to_all | solution.py:13
  120.6 1.1 reduce_sum.64
  121.9 17.2 %all_to_all.48 = f32[64,1,1024]{2,1,0:T(1,128)S(1)} all-to-all(f32[64,1,1024]{2,1,0:T(1,128)S(1)} %broadcast_in_dim.20), channel_id=1, replica_groups=mesh['tok'=64,'feat'=8] {'tok'}, dimensions={0} | all-to-all | bytes 524288 | tf_op jit(solution)/shard_map/all_to_all | solution.py:13
  139.8 1.7 fusion.16
  141.5 17.6 %all_to_all.49 = f32[8,64,128]{2,1,0:T(8,128)} all-to-all(f32[8,64,128]{2,1,0:T(8,128)S(1)} %broadcast_in_dim.21), channel_id=1, replica_groups=mesh['tok'=64,'feat'=8] {'feat'}, dimensions={0} | all-to-all | bytes 524288 | tf_op jit(solution)/shard_map/all_to_all | solution.py:13
  159.1 1.6 reduce_sum.65
  160.6 1.4 fusion
  162.1 2.5 fusion.2
  164.6 2.0 fusion.39
  166.6 2.0 fusion.35
  168.5 2.0 fusion.37
  170.5 2.0 concatenate.65
  172.5 24.0 %all_to_all.50 = f32[8,8,2432]{2,1,0:T(8,128)} all-to-all(f32[8,8,2432]{2,1,0:T(8,128)} %bitcast.123), channel_id=1, replica_groups=mesh['tok'=64,'feat'=8] {'feat'}, dimensions={0} | all-to-all | bytes 1245184 | tf_op jit(solution)/shard_map/all_to_all | solution.py:13
  196.5 1.7 reduce_sum.66
  198.3 0.9 convert_element_type.38
  200.0 16.7 %all_to_all.51 = bf16[8,8,2624]{2,1,0:T(8,128)(2,1)S(1)} all-to-all(bf16[8,8,2624]{2,1,0:T(8,128)(2,1)S(1)} %broadcast_in_dim.22), channel_id=1, replica_groups=mesh['tok'=64,'feat'=8] {'feat'}, dimensions={0} | all-to-all | bytes 671744 | tf_op jit(solution)/shard_map/all_to_all | solution.py:13
  218.3 3.5 %reduce_sum.67 = f32[64,2432]{1,0:T(8,128)} reduce(f32[8,64,2432]{2,1,0:T(8,128)} %bitcast.120, f32[]{:T(128)} %constant.6.clone.1), dimensions={0}, to_apply=%region_4.0 | reduce | flops 1089536 | bytes 5603332 | tf_op jit(solution)/shard_map/reduce_sum | solution.py:62
  221.9 1.3 fusion.8
  223.1 1.0 slice.205
  224.2 1.6 fusion.17
  226.3 1.4 copy.48
  227.7 5.7 %all-to-all-start.7 = ((f32[64,1,2240]{2,1,0:T(1,128)}), f32[64,1,2240]{2,1,0:T(1,128)S(1)}, u32[]{:S(2)}, u32[]{:S(2)}) async-start(f32[64,1,2240]{2,1,0:T(1,128)} %copy.48), calls=%async_computation.7 | async-start | bytes 1179648 | tf_op jit(solution)/shard_map/all_to_all | solution.py:13
  233.7 0.9 slice_convert_fusion.2
  234.6 17.5 %all-to-all-done.7 = f32[64,1,2240]{2,1,0:T(1,128)S(1)} async-done(((f32[64,1,2240]{2,1,0:T(1,128)}), f32[64,1,2240]{2,1,0:T(1,128)S(1)}, u32[]{:S(2)}, u32[]{:S(2)}) %all-to-all-start.7) | async-done | bytes 573472 | tf_op jit(solution)/shard_map/all_to_all | solution.py:13
  252.5 1.1 broadcast_in_dim.24
  253.6 6.3 %all-to-all-start.8 = ((f32[64,1,2240]{2,1,0:T(1,128)}), f32[64,1,2240]{2,1,0:T(1,128)S(1)}, u32[]{:S(2)}, u32[]{:S(2)}) async-start(f32[64,1,2240]{2,1,0:T(1,128)} %broadcast_in_dim.24), calls=%async_computation.8 | async-start | bytes 1179648 | tf_op jit(solution)/shard_map/all_to_all | solution.py:13
  260.5 0.9 fusion.48
  261.7 16.2 %all-to-all-done.8 = f32[64,1,2240]{2,1,0:T(1,128)S(1)} async-done(((f32[64,1,2240]{2,1,0:T(1,128)}), f32[64,1,2240]{2,1,0:T(1,128)S(1)}, u32[]{:S(2)}, u32[]{:S(2)}) %all-to-all-start.8) | async-done | bytes 573472 | tf_op jit(solution)/shard_map/all_to_all | solution.py:13
  278.7 0.8 copy.60
  279.5 0.9 maximum_bitcast_fusion
  (67 shorter events, 9.3 us)
Async XLA Ops:
  7.2 14.6 %copy-start = (bf16[1728,1024]{1,0:T(8,128)(2,1)S(1)}, bf16[1728,1024]{1,0:T(8,128)(2,1)}, u32[]{:S(2)}) copy-start(bf16[1728,1024]{1,0:T(8,128)(2,1)} %param.3) | copy-start | bytes 10616836
  7.2 211.1 %all-gather.3.cloned.1.call-start = ((), (), s32[]{:S(2)}) async-start(), calls=%async_computation.9 | async-start | bytes 5603328 | tf_op jit(solution)/shard_map/all_gather | solution.py:62
  7.2 14.5 %copy-start.1 = (f32[1024,64]{0,1:T(8,128)S(1)}, f32[1024,64]{0,1:T(8,128)}, u32[]{:S(2)}) copy-start(f32[1024,64]{0,1:T(8,128)} %param.4) | copy-start | bytes 786436
  8.7 18.6 %collective-permute-start.1 = (bf16[256,1024]{1,0:T(8,128)(2,1)S(1)}, bf16[256,1024]{1,0:T(8,128)(2,1)S(1)}, u32[]{:S(2)}, u32[]{:S(2)}) collective-permute-start(bf16[256,1024]{1,0:T(8,128)(2,1)S(1)} %get-tuple-element.16), channel_id=1, source_target_pairs={{0,8},{8,16},{16,24},{24,32},{32,40},{40,48},{48,56},{56,64},{64,7... | collective-permute-start | bytes 1572872 | tf_op jit(solution)/shard_map/ppermute | solution.py:38
  12.1 11.7 %copy-start.2 = (f32[1024,64]{0,1:T(8,128)S(1)}, f32[1024,64]{0,1:T(8,128)}, u32[]{:S(2)}) copy-start(f32[1024,64]{0,1:T(8,128)} %param.5) | copy-start | bytes 786436
  12.1 16.9 %collective-permute-start = (bf16[256,1024]{1,0:T(8,128)(2,1)S(1)}, bf16[256,1024]{1,0:T(8,128)(2,1)S(1)}, u32[]{:S(2)}, u32[]{:S(2)}) collective-permute-start(bf16[256,1024]{1,0:T(8,128)(2,1)S(1)} %get-tuple-element.15), channel_id=1, source_target_pairs={{8,0},{16,8},{24,16},{32,24},{40,32},{48,40},{56,48},{64,56},{72,6... | collective-permute-start | bytes 1572872 | tf_op jit(solution)/shard_map/ppermute | solution.py:39
  27.2 0.8 copy-start.3
  28.9 0.8 copy-start.4
  139.1 0.7 copy-start.5
  216.7 0.8 copy-start.7
  221.8 3.9 %copy-start.8 = (bf16[64,1728]{1,0:T(8,128)(2,1)S(1)}, bf16[64,1728]{1,0:T(8,128)(2,1)}, u32[]{:S(2)}) copy-start(bf16[64,1728]{1,0:T(8,128)(2,1)} %fusion.9) | copy-start | bytes 663556
  221.8 3.9 %copy-start.10 = (bf16[64,1728]{1,0:T(8,128)(2,1)S(1)}, bf16[64,1728]{1,0:T(8,128)(2,1)}, u32[]{:S(2)}) copy-start(bf16[64,1728]{1,0:T(8,128)(2,1)} %slice.152) | copy-start | bytes 663556
  225.8 7.7 %copy-start.6 = (f32[64,1,1024]{2,1,0:T(1,128)S(1)}, f32[64,1,1024]{2,1,0:T(1,128)}, u32[]{:S(2)}) copy-start(f32[64,1,1024]{2,1,0:T(1,128)} %copy-done.5) | copy-start | bytes 786436
  225.8 7.7 %copy-start.9 = (f32[64,128]{1,0:T(8,128)S(1)}, f32[64,128]{1,0:T(8,128)}, u32[]{:S(2)}) copy-start(f32[64,128]{1,0:T(8,128)} %reduce_sum.65) | copy-start | bytes 98308
  227.7 24.4 %all-to-all-start.7 = ((f32[64,1,2240]{2,1,0:T(1,128)}), f32[64,1,2240]{2,1,0:T(1,128)S(1)}, u32[]{:S(2)}, u32[]{:S(2)}) async-start(f32[64,1,2240]{2,1,0:T(1,128)} %copy.48), calls=%async_computation.7 | async-start | bytes 1179648 | tf_op jit(solution)/shard_map/all_to_all | solution.py:13
  253.6 24.2 %all-to-all-start.8 = ((f32[64,1,2240]{2,1,0:T(1,128)}), f32[64,1,2240]{2,1,0:T(1,128)S(1)}, u32[]{:S(2)}, u32[]{:S(2)}) async-start(f32[64,1,2240]{2,1,0:T(1,128)} %broadcast_in_dim.24), calls=%async_computation.8 | async-start | bytes 1179648 | tf_op jit(solution)/shard_map/all_to_all | solution.py:13
Sparse Core Ops, SparseCore 0:
  32.8 75.7 all-gather.2
